TPU v7x, 512 devices: a whole 4x4x16 slice. The times are simulated.
512 devices in a mesh: gx: 8 (over z_lo), gy: 4 (over z_hi, core), gz: 16 (over y, x).
Axes of the slice: x: 4, y: 4, z: 16 (z_hi: 2, z_lo: 8; z = z_hi * 8 + z_lo), core: 2. Of those that a mesh axis runs over, the one named last changes fastest.
Arguments:
- probe_vectors: float32 [32, 16, 32, 2048], P(None, 'gx', 'gy', 'gz'), may hold values from -6 to 6
- layer_ids: int32 [16, 32, 2048], P('gx', 'gy', 'gz'), may hold values from 0 to 15
- layer_kappa: float32 [16], replicated, may hold values from 0.1 to 10
- slot_order: int32 [32, 16], replicated, may hold values from 0 to 511, as said below
Outputs:
- factored: float32 [16384, 16384], P(('gx', 'gy'), 'gz')
Inputs may be any that keep to these rules, and one draw needn't show every extreme that they name: `slot_order`: the entries are an ordering of 0 to 511, and in each column the entries divided by 16, rounded down, are an ordering of 0 to 31.
All inputs are finite; a program needn't handle non-finite values.
Results may differ from a plain program's by a relative error of at most 0.00013.
Values sent between devices are 32-bit elements; how exact they have to be, the bound alone decides.
No kernel may reach another device: no remote copies, remote signals or barrier semaphores. Data moves between devices by JAX's collectives and lax.ppermute only.
A program may use at most 128 MiB of HBM per device.

v0:
```python
import math
import jax
import jax.numpy as jnp
from jax import lax
from jax.sharding import PartitionSpec as P

PASSES = 4
PANEL = 256
NPAN = 2
upper_edge = 120.0
lower_edge = 24.0
coarse_shift = 1.0


def with_halo(block, sides, width):
    for axis, dim in sides:
        count = lax.axis_size(axis)
        forward = [(i, i + 1) for i in range(count - 1)]
        backward = [(target, source) for source, target in forward]
        low = lax.ppermute(
            lax.slice_in_dim(block, block.shape[dim] - width, None, axis=dim), axis, forward
        )
        high = lax.ppermute(lax.slice_in_dim(block, 0, width, axis=dim), axis, backward)
        block = jnp.concatenate([low, block, high], axis=dim)
    return block


def from_root(value, axis, source):
    kept = jnp.where(lax.axis_index(axis) == source, value, 0).astype(value.dtype)
    return lax.psum(kept, axis)


def cheb_factors(step_index):
    center = (upper_edge + lower_edge) / (upper_edge - lower_edge)
    growth = math.log(center + math.sqrt(center * center - 1.0))

    def chebval(degree):
        expo = math.exp(degree * growth)
        return 0.5 * (expo + 1.0 / expo)

    if step_index == 0:
        return (1.0 / chebval(1), 0.0)
    return (
        2.0 * chebval(step_index) / chebval(step_index + 1),
        chebval(step_index - 1) / chebval(step_index + 1),
    )


def face_weights(kappa_pad):
    center = kappa_pad[1:-1, 1:-1, 1:-1]
    x_plus = 0.5 * (center + kappa_pad[2:, 1:-1, 1:-1])
    x_minus = 0.5 * (center + kappa_pad[:-2, 1:-1, 1:-1])
    y_plus = 0.5 * (center + kappa_pad[1:-1, 2:, 1:-1])
    y_minus = 0.5 * (center + kappa_pad[1:-1, :-2, 1:-1])
    z_plus = 0.5 * (center + kappa_pad[1:-1, 1:-1, 2:])
    z_minus = 0.5 * (center + kappa_pad[1:-1, 1:-1, :-2])
    diagonal = x_plus + x_minus + y_plus + y_minus + z_plus + z_minus
    return ((x_plus, x_minus, y_plus, y_minus, z_plus, z_minus), diagonal)


def apply_operator(field_pad, weights, diagonal):
    x_plus, x_minus, y_plus, y_minus, z_plus, z_minus = weights
    interior = field_pad[..., 1:-1, 1:-1, 1:-1]
    beside = x_plus * field_pad[..., 2:, 1:-1, 1:-1] + x_minus * field_pad[..., :-2, 1:-1, 1:-1]
    beside = (
        beside + y_plus * field_pad[..., 1:-1, 2:, 1:-1] + y_minus * field_pad[..., 1:-1, :-2, 1:-1]
    )
    beside = (
        beside + z_plus * field_pad[..., 1:-1, 1:-1, 2:] + z_minus * field_pad[..., 1:-1, 1:-1, :-2]
    )
    return diagonal * interior - beside


def cheb_update(current, previous, applied, step_index):
    factor_one, factor_two = cheb_factors(step_index)
    shifted = (upper_edge + lower_edge) / (upper_edge - lower_edge) * current - 2.0 / (
        upper_edge - lower_edge
    ) * applied
    return factor_one * shifted - factor_two * previous


def face_block(own_face, weight_face, ghost_face, scaling):
    return -scaling * jnp.einsum(
        "kab,ab,lab->kl", own_face, weight_face, ghost_face, precision=lax.Precision.HIGHEST
    )


def table_lookup(table, row_wanted, col_wanted):
    row_ids = jnp.arange(table.shape[0], dtype=jnp.int32)
    col_ids = jnp.arange(table.shape[1], dtype=jnp.int32)
    hit = (row_wanted[..., None, None] == row_ids[:, None]) & (
        col_wanted[..., None, None] == col_ids[None, :]
    )
    return jnp.sum(jnp.where(hit, table, 0), axis=(-2, -1))


def on_device(probe_vectors, layer_ids, layer_kappa, slot_order):
    highest = lax.Precision.HIGHEST
    grid_x = lax.axis_size("gx")
    grid_y = lax.axis_size("gy")
    grid_z = lax.axis_size("gz")
    index_x = lax.axis_index("gx")
    index_y = lax.axis_index("gy")
    index_z = lax.axis_index("gz")
    vectors, extent_x, extent_y, extent_z = probe_vectors.shape
    layers = layer_kappa.shape[0]
    choose = layer_ids[None] == jnp.arange(layers, dtype=jnp.int32)[:, None, None, None]
    conductivity = jnp.sum(jnp.where(choose, layer_kappa[:, None, None, None], 0.0), axis=0)
    kappa_pad = with_halo(conductivity, (("gx", 0), ("gy", 1), ("gz", 2)), 1)
    weights, diagonal = face_weights(kappa_pad)
    current = probe_vectors
    previous = jnp.zeros_like(probe_vectors)
    for step_index in range(PASSES):
        padded = with_halo(current, (("gx", 1), ("gy", 2), ("gz", 3)), 1)
        applied = apply_operator(padded, weights, diagonal)
        current, previous = (cheb_update(current, previous, applied, step_index), current)
    ghosts = with_halo(current, (("gx", 1), ("gy", 2), ("gz", 3)), 1)
    local_image = apply_operator(
        jnp.pad(current, ((0, 0), (1, 1), (1, 1), (1, 1))), weights, diagonal
    )
    cell_count = extent_x * extent_y * extent_z
    scaling = 1.0 / math.sqrt(cell_count)
    flattened = current.reshape(vectors, cell_count)
    own_block = scaling * jnp.dot(
        flattened, local_image.reshape(vectors, cell_count).T, precision=highest
    )
    own_block = own_block + coarse_shift * jnp.eye(vectors, dtype=jnp.float32)
    x_plus, x_minus, y_plus, y_minus, z_plus, z_minus = weights
    blocks = jnp.stack(
        [
            own_block,
            face_block(current[:, 0], x_minus[0], ghosts[:, 0, 1:-1, 1:-1], scaling),
            face_block(current[:, -1], x_plus[-1], ghosts[:, -1, 1:-1, 1:-1], scaling),
            face_block(current[:, :, 0], y_minus[:, 0], ghosts[:, 1:-1, 0, 1:-1], scaling),
            face_block(current[:, :, -1], y_plus[:, -1], ghosts[:, 1:-1, -1, 1:-1], scaling),
            face_block(current[:, :, :, 0], z_minus[:, :, 0], ghosts[:, 1:-1, 1:-1, 0], scaling),
            face_block(current[:, :, :, -1], z_plus[:, :, -1], ghosts[:, 1:-1, 1:-1, -1], scaling),
        ]
    )
    rows_total = grid_x * grid_y
    row_index = index_x * grid_y + index_y
    row_ids = jnp.arange(rows_total, dtype=jnp.int32)
    group_of = slot_order // grid_z
    column_groups = lax.dynamic_index_in_dim(group_of, index_z, 1, keepdims=False)
    owner_source = jnp.sum(jnp.where(column_groups == row_index, row_ids, 0))
    piece = lax.all_gather(blocks[None], ("gx", "gy"), axis=0, tiled=True)
    anchor = jnp.arange(piece.shape[0], dtype=jnp.int32)
    wanted = (anchor == owner_source)[:, None, None, None]
    owned = jnp.sum(jnp.where(wanted, piece, 0.0), axis=0)
    sources = jnp.arange(grid_z, dtype=jnp.int32)
    source_rows = jnp.sum(jnp.where(group_of == row_index, row_ids[:, None], 0), axis=0)
    source_x = source_rows // grid_y
    source_y = source_rows % grid_y
    neighbour_rows = jnp.stack(
        [
            source_rows,
            source_rows - grid_y,
            source_rows + grid_y,
            source_rows - 1,
            source_rows + 1,
            source_rows,
            source_rows,
        ],
        axis=1,
    )
    neighbour_cols = jnp.stack(
        [sources, sources, sources, sources, sources, sources - 1, sources + 1], axis=1
    )
    always = jnp.ones((grid_z,), bool)
    usable = jnp.stack(
        [
            always,
            source_x > 0,
            source_x < grid_x - 1,
            source_y > 0,
            source_y < grid_y - 1,
            sources > 0,
            sources < grid_z - 1,
        ],
        axis=1,
    )
    targets = table_lookup(slot_order, neighbour_rows, neighbour_cols)
    own_slots = table_lookup(slot_order, source_rows, sources) - row_index * grid_z
    local_cols = targets - index_z * rows_total
    usable = usable & (local_cols >= 0) & (local_cols < rows_total)
    col_flat = jnp.where(usable, local_cols, rows_total).reshape(-1)
    row_flat = jnp.broadcast_to(own_slots[:, None], (grid_z, 7)).reshape(-1)
    empty_grid = jnp.zeros((grid_z, vectors, rows_total, vectors), jnp.float32)
    gathered = empty_grid.at[row_flat, :, col_flat, :].add(
        lax.all_gather(owned, "gz", axis=0, tiled=True), mode="drop"
    )
    coarse = gathered.reshape(grid_z * vectors, rows_total * vectors)
    rows_local = coarse.shape[0]
    cols_local = coarse.shape[1]
    panel_width = min(PANEL, rows_local, cols_local)
    global_rows = row_index * rows_local + jnp.arange(rows_local, dtype=jnp.int32)
    global_cols = index_z * cols_local + jnp.arange(cols_local, dtype=jnp.int32)
    offsets = jnp.arange(panel_width, dtype=jnp.int32)
    for panel_index in range(NPAN):
        panel_begin = panel_index * panel_width
        panel_end = panel_begin + panel_width
        row_root = panel_begin // rows_local
        col_root = panel_begin // cols_local
        row_start = panel_begin - row_root * rows_local
        col_start = panel_begin - col_root * cols_local
        column_piece = from_root(coarse[:, col_start : col_start + panel_width], "gz", col_root)
        row_piece, diagonal_piece = (
            from_root(coarse[row_start : row_start + panel_width, :], ("gx", "gy"), row_root),
            from_root(column_piece[row_start : row_start + panel_width, :], ("gx", "gy"), row_root),
        )
        factor = jnp.linalg.cholesky(diagonal_piece)
        row_factor = jax.scipy.linalg.solve_triangular(factor, column_piece.T, lower=True).T
        col_factor = jax.scipy.linalg.solve_triangular(factor, row_piece, lower=True).T
        row_factor = jnp.where(
            global_rows[:, None] >= panel_begin + offsets[None, :], row_factor, 0.0
        )
        updated = coarse - jnp.dot(row_factor, col_factor.T, precision=highest)
        trail_rows = global_rows >= panel_end
        trail_cols = global_cols >= panel_end
        panel_rows = (global_rows >= panel_begin) & (global_rows < panel_end)
        coarse = jnp.where(
            trail_rows[:, None] & trail_cols[None, :],
            updated,
            jnp.where(panel_rows[:, None] & trail_cols[None, :], 0.0, coarse),
        )
        old_columns = coarse[:, col_start : col_start + panel_width]
        new_columns = jnp.where(index_z == col_root, row_factor, old_columns)
        coarse = coarse.at[:, col_start : col_start + panel_width].set(new_columns)
    return coarse


def solution(mesh):
    in_specs = (P(None, "gx", "gy", "gz"), P("gx", "gy", "gz"), P(), P())
    out_specs = P(("gx", "gy"), "gz")
    return jax.shard_map(
        on_device, mesh=mesh, in_specs=in_specs, out_specs=out_specs, check_vma=False
    )
```

profile of v0, /device:TPU:1, one launch (start us, length us, event | category | flops | bytes accessed | tf_op | source)
XLA Modules:
  0.0 1363.8 jit_solution(13902177501467770364)
XLA Ops:
  8.7 5.0 collective-permute-start.1
  14.7 3.6 collective-permute-start.7
  20.8 3.0 select_reduce_fusion.1
  23.9 15.8 %collective-permute-start.3 = (f32[4,1,128]{2,1,0:T(1,128)S(1)}, f32[4,1,128]{2,1,0:T(1,128)S(1)}, u32[]{:S(2)}, u32[]{:S(2)}) collective-permute-start(f32[4,1,128]{2,1,0:T(1,128)S(1)} %get-tuple-element.143), channel_id=1, source_target_pairs={{0,16},{16,32},{32,48},{1,17},{17,33},{33,49},{2,18},{18,34},{34,5... | collective-permute-start | bytes 6152 | tf_op jit(solution)/shard_map/ppermute | solution.py:20
  39.7 1.9 collective-permute-start.2
  41.7 11.6 collective-permute-done.2
  54.7 4.0 collective-permute-start.5
  60.8 1.9 collective-permute-start.8
  62.7 12.4 collective-permute-start.9
  78.7 4.3 collective-permute-start.11
  85.8 4.8 collective-permute-start.13
  91.1 1.4 collective-permute-done.13
  92.6 1.9 collective-permute-start.14
  94.5 14.7 %collective-permute-start.15 = (f32[32,4,1,128]{3,0,2,1:T(8,128)S(1)}, f32[32,4,1,128]{3,0,2,1:T(8,128)S(1)}, u32[]{:S(2)}, u32[]{:S(2)}) collective-permute-start(f32[32,4,1,128]{3,0,2,1:T(8,128)S(1)} %get-tuple-element.117), channel_id=1, source_target_pairs={{0,16},{16,32},{32,48},{1,17},{17,33},{33,49},{2,18},{18,34},{34,5... | collective-permute-start | bytes 196616 | tf_op jit(solution)/shard_map/ppermute | solution.py:20
  109.4 1.5 collective-permute-done.15
  113.1 4.6 collective-permute-start.17
  121.1 5.0 collective-permute-start.19
  126.5 1.5 collective-permute-done.19
  128.1 1.9 collective-permute-start.20
  130.0 14.2 %collective-permute-start.21 = (f32[32,4,1,128]{3,0,2,1:T(8,128)S(1)}, f32[32,4,1,128]{3,0,2,1:T(8,128)S(1)}, u32[]{:S(2)}, u32[]{:S(2)}) collective-permute-start(f32[32,4,1,128]{3,0,2,1:T(8,128)S(1)} %get-tuple-element.115), channel_id=1, source_target_pairs={{0,16},{16,32},{32,48},{1,17},{17,33},{33,49},{2,18},{18,34},{34,5... | collective-permute-start | bytes 196616 | tf_op jit(solution)/shard_map/ppermute | solution.py:20
  147.7 4.5 collective-permute-start.23
  155.2 4.7 collective-permute-start.25
  160.3 1.5 collective-permute-done.25
  161.9 1.9 collective-permute-start.26
  163.8 15.1 %collective-permute-start.27 = (f32[32,4,1,128]{3,0,2,1:T(8,128)S(1)}, f32[32,4,1,128]{3,0,2,1:T(8,128)S(1)}, u32[]{:S(2)}, u32[]{:S(2)}) collective-permute-start(f32[32,4,1,128]{3,0,2,1:T(8,128)S(1)} %get-tuple-element.113), channel_id=1, source_target_pairs={{0,16},{16,32},{32,48},{1,17},{17,33},{33,49},{2,18},{18,34},{34,5... | collective-permute-start | bytes 196616 | tf_op jit(solution)/shard_map/ppermute | solution.py:20
  182.4 4.9 collective-permute-start.29
  189.0 6.5 collective-permute-start.30
  197.7 6.0 collective-permute-done.31
  203.7 15.1 %collective-permute-start.32 = (f32[32,4,1,128]{3,0,2,1:T(8,128)S(1)}, f32[32,4,1,128]{3,0,2,1:T(8,128)S(1)}, u32[]{:S(2)}, u32[]{:S(2)}) collective-permute-start(f32[32,4,1,128]{3,0,2,1:T(8,128)S(1)} %get-tuple-element.112), channel_id=1, source_target_pairs={{0,16},{16,32},{32,48},{1,17},{17,33},{33,49},{2,18},{18,34},{34,5... | collective-permute-start | bytes 196616 | tf_op jit(solution)/shard_map/ppermute | solution.py:20
  218.8 2.1 collective-permute-start.33
  221.5 12.0 collective-permute-done.33
  234.1 6.0 collective-permute-start.34
  242.3 5.3 collective-permute-done.35
  247.8 212.4 %all-gather = f32[224,32,32]{2,1,0:T(8,128)S(1)} all-gather(f32[7,32,32]{2,1,0:T(8,128)S(1)} %fusion.2), channel_id=2, replica_groups=mesh['gx'=8,'gy'=4,'gz'=16] {'gx','gy'}, dimensions={0}, use_global_device_ids=true | all-gather | bytes 946176 | tf_op jit(solution)/shard_map/all_gather | solution.py:146
  460.7 50.5 %all_gather.7 = f32[112,32,32]{2,1,0:T(8,128)S(1)} all-gather(f32[7,32,32]{2,1,0:T(8,128)S(1)} %select_reduce_fusion), channel_id=1, replica_groups=mesh['gx'=8,'gy'=4,'gz'=16] {'gz'}, dimensions={0}, use_global_device_ids=true | all-gather | bytes 487424 | tf_op jit(solution)/shard_map/all_gather | solution.py:190
  511.2 4.3 broadcast_in_dim.82
  515.5 16.4 %scatter_fusion = f32[16,32,32,32]{3,1,2,0:T(8,128)} fusion(f32[16,32,32,32]{3,1,2,0:T(8,128)} %broadcast_in_dim.82, s32[112]{0:T(128)S(1)} %fusion.191, f32[112,32,32]{2,1,0:T(8,128)S(1)} %all_gather.7), kind=kCustom, calls=%fused_computation | custom fusion | flops 114688 | bytes 1377152 | tf_op jit(solution)/shard_map/scatter-add | solution.py:189
  531.9 9.0 copy.208
  540.9 6.2 reshape.408
  548.2 3.0 slice_select_fusion
  551.2 4.3 copy.210
  555.5 4.6 select_n.194
  560.1 101.7 %all-reduce.9.cloned.1.call-done = f32[512,256]{0,1:T(8,128)} async-done(((f32[512,256]{0,1:T(8,128)}), f32[512,256]{0,1:T(8,128)}) %all-reduce.9.cloned.1.call-update) | async-done | bytes 524304 | tf_op jit(solution)/shard_map/psum | solution.py:30
  661.8 1.7 slice_select_fusion.5
  664.6 214.9 %all-reduce.15.cloned.1.call-done = (f32[256,1024]{1,0:T(8,128)}, f32[256,256]{0,1:T(8,128)}) async-done(((f32[256,1024]{1,0:T(8,128)}, f32[256,256]{0,1:T(8,128)}), (f32[256,1024]{1,0:T(8,128)}, f32[256,256]{0,1:T(8,128)})) %all-reduce.15.cloned.1.call-update) | async-done | bytes 1310736 | tf_op jit(solution)/shard_map/psum | solution.py:30
  881.6 11.7 cholesky.130
  893.3 9.8 custom-call.19
  903.6 11.7 cholesky.147
  918.2 4.0 while.10
  922.2 19.8 %custom-call.20 = f32[2,128,128]{1,2,0:T(8,128)S(1)} custom-call(f32[2,128,128]{2,1,0:T(8,128)S(1)} %get-tuple-element.60), custom_call_target="InvertDiagBlocksLowerTriangular" | custom-call | tf_op jit(solution)/shard_map/jit(_solve_triangular)/triangular_solve | solution.py:212
  945.2 2.7 select_select_fusion.1
  950.6 113.2 %all-reduce.11.cloned.1.call-done = f32[512,256]{0,1:T(8,128)} async-done(((f32[512,256]{0,1:T(8,128)}), f32[512,256]{0,1:T(8,128)}) %all-reduce.11.cloned.1.call-update) | async-done | bytes 524304 | tf_op jit(solution)/shard_map/psum | solution.py:30
  1063.8 1.7 slice_select_fusion.4
  1066.4 214.9 %all-reduce.13.cloned.1.call-done = (f32[256,1024]{0,1:T(8,128)}, f32[256,256]{0,1:T(8,128)}) async-done(((f32[256,1024]{0,1:T(8,128)}, f32[256,256]{0,1:T(8,128)}), (f32[256,1024]{0,1:T(8,128)}, f32[256,256]{0,1:T(8,128)})) %all-reduce.13.cloned.1.call-update) | async-done | bytes 1310736 | tf_op jit(solution)/shard_map/psum | solution.py:30
  1283.5 11.7 cholesky.164
  1295.2 9.8 custom-call.22
  1305.5 11.7 cholesky.181
  1319.9 4.0 while.11
  1320.5 1.4 bitcast_dynamic-update-slice_fusion.5
  1322.5 1.4 bitcast_dynamic-update-slice_fusion.5
  1323.9 19.9 %custom-call.23 = f32[2,128,128]{1,2,0:T(8,128)S(1)} custom-call(f32[2,128,128]{2,1,0:T(8,128)S(1)} %get-tuple-element.62), custom_call_target="InvertDiagBlocksLowerTriangular" | custom-call | tf_op jit(solution)/shard_map/jit(_solve_triangular)/triangular_solve | solution.py:212
  1347.4 3.9 select_select_fusion
  1351.3 2.6 fusion.29
  1354.0 2.9 copy.215
  (224 shorter events, 65.8 us)
Async XLA Ops:
  6.5 655.2 %all-reduce.9.cloned.1.call-start = ((), (), s32[]{:S(2)}) async-start(), calls=%async_computation | async-start | bytes 1048576 | tf_op jit(solution)/shard_map/psum | solution.py:30
  7.3 16.5 %collective-permute-start = (f32[1,8,128]{2,1,0:T(8,128)S(1)}, f32[1,8,128]{2,1,0:T(8,128)S(1)}, u32[]{:S(2)}, u32[]{:S(2)}) collective-permute-start(f32[1,8,128]{2,1,0:T(8,128)S(1)} %get-tuple-element.146), channel_id=1, source_target_pairs={{64,0},{128,64},{192,128},{256,192},{320,256},{384,320},{448,384},... | collective-permute-start | bytes 12296 | tf_op jit(solution)/shard_map/ppermute | solution.py:23
  8.7 15.2 %collective-permute-start.1 = (f32[1,8,128]{2,1,0:T(8,128)S(1)}, f32[1,8,128]{2,1,0:T(8,128)S(1)}, u32[]{:S(2)}, u32[]{:S(2)}) collective-permute-start(f32[1,8,128]{2,1,0:T(8,128)S(1)} %get-tuple-element.145), channel_id=1, source_target_pairs={{0,64},{64,128},{128,192},{192,256},{256,320},{320,384},{384,448},... | collective-permute-start | bytes 12296 | tf_op jit(solution)/shard_map/ppermute | solution.py:20
  14.7 45.0 %collective-permute-start.7 = (f32[32,1,8,128]{3,0,2,1:T(8,128)S(1)}, f32[32,1,8,128]{3,0,2,1:T(8,128)S(1)}, u32[]{:S(2)}, u32[]{:S(2)}) collective-permute-start(f32[32,1,8,128]{3,0,2,1:T(8,128)S(1)} %get-tuple-element.130), channel_id=1, source_target_pairs={{0,64},{64,128},{128,192},{192,256},{256,320},{320,384},{384,448},... | collective-permute-start | bytes 393224 | tf_op jit(solution)/shard_map/ppermute | solution.py:20
  18.3 42.5 %collective-permute-start.6 = (f32[32,1,8,128]{3,0,2,1:T(8,128)S(1)}, f32[32,1,8,128]{3,0,2,1:T(8,128)S(1)}, u32[]{:S(2)}, u32[]{:S(2)}) collective-permute-start(f32[32,1,8,128]{3,0,2,1:T(8,128)S(1)} %get-tuple-element.129), channel_id=1, source_target_pairs={{64,0},{128,64},{192,128},{256,192},{320,256},{384,320},{448,384},... | collective-permute-start | bytes 393224 | tf_op jit(solution)/shard_map/ppermute | solution.py:23
  23.9 17.7 %collective-permute-start.3 = (f32[4,1,128]{2,1,0:T(1,128)S(1)}, f32[4,1,128]{2,1,0:T(1,128)S(1)}, u32[]{:S(2)}, u32[]{:S(2)}) collective-permute-start(f32[4,1,128]{2,1,0:T(1,128)S(1)} %get-tuple-element.143), channel_id=1, source_target_pairs={{0,16},{16,32},{32,48},{1,17},{17,33},{33,49},{2,18},{18,34},{34,5... | collective-permute-start | bytes 6152 | tf_op jit(solution)/shard_map/ppermute | solution.py:20
  39.7 13.6 collective-permute-start.2
  53.4 5.4 collective-permute-start.4
  54.7 4.9 collective-permute-start.5
  60.8 14.4 %collective-permute-start.8 = (f32[32,4,1,128]{3,0,2,1:T(8,128)S(1)}, f32[32,4,1,128]{3,0,2,1:T(8,128)S(1)}, u32[]{:S(2)}, u32[]{:S(2)}) collective-permute-start(f32[32,4,1,128]{3,0,2,1:T(8,128)S(1)} %get-tuple-element.120), channel_id=1, source_target_pairs={{16,0},{32,16},{48,32},{17,1},{33,17},{49,33},{18,2},{34,18},{50,3... | collective-permute-start | bytes 196616 | tf_op jit(solution)/shard_map/ppermute | solution.py:23
  62.7 13.8 %collective-permute-start.9 = (f32[32,4,1,128]{3,0,2,1:T(8,128)S(1)}, f32[32,4,1,128]{3,0,2,1:T(8,128)S(1)}, u32[]{:S(2)}, u32[]{:S(2)}) collective-permute-start(f32[32,4,1,128]{3,0,2,1:T(8,128)S(1)} %get-tuple-element.119), channel_id=1, source_target_pairs={{0,16},{16,32},{32,48},{1,17},{17,33},{33,49},{2,18},{18,34},{34,5... | collective-permute-start | bytes 196616 | tf_op jit(solution)/shard_map/ppermute | solution.py:20
  77.1 5.9 collective-permute-start.10
  78.7 5.2 collective-permute-start.11
  83.3 7.4 copy-start.7
  84.5 6.6 collective-permute-start.12
  85.8 6.8 collective-permute-start.13
  92.6 16.8 %collective-permute-start.14 = (f32[32,4,1,128]{3,0,2,1:T(8,128)S(1)}, f32[32,4,1,128]{3,0,2,1:T(8,128)S(1)}, u32[]{:S(2)}, u32[]{:S(2)}) collective-permute-start(f32[32,4,1,128]{3,0,2,1:T(8,128)S(1)} %get-tuple-element.118), channel_id=1, source_target_pairs={{16,0},{32,16},{48,32},{17,1},{33,17},{49,33},{18,2},{34,18},{50,3... | collective-permute-start | bytes 196616 | tf_op jit(solution)/shard_map/ppermute | solution.py:23
  94.5 16.3 %collective-permute-start.15 = (f32[32,4,1,128]{3,0,2,1:T(8,128)S(1)}, f32[32,4,1,128]{3,0,2,1:T(8,128)S(1)}, u32[]{:S(2)}, u32[]{:S(2)}) collective-permute-start(f32[32,4,1,128]{3,0,2,1:T(8,128)S(1)} %get-tuple-element.117), channel_id=1, source_target_pairs={{0,16},{16,32},{32,48},{1,17},{17,33},{33,49},{2,18},{18,34},{34,5... | collective-permute-start | bytes 196616 | tf_op jit(solution)/shard_map/ppermute | solution.py:20
  110.9 8.5 copy-start.2
  111.5 7.3 collective-permute-start.16
  113.1 6.0 collective-permute-start.17
  119.8 6.7 collective-permute-start.18
  121.1 6.9 collective-permute-start.19
  128.1 16.8 %collective-permute-start.20 = (f32[32,4,1,128]{3,0,2,1:T(8,128)S(1)}, f32[32,4,1,128]{3,0,2,1:T(8,128)S(1)}, u32[]{:S(2)}, u32[]{:S(2)}) collective-permute-start(f32[32,4,1,128]{3,0,2,1:T(8,128)S(1)} %get-tuple-element.116), channel_id=1, source_target_pairs={{16,0},{32,16},{48,32},{17,1},{33,17},{49,33},{18,2},{34,18},{50,3... | collective-permute-start | bytes 196616 | tf_op jit(solution)/shard_map/ppermute | solution.py:23
  130.0 15.6 %collective-permute-start.21 = (f32[32,4,1,128]{3,0,2,1:T(8,128)S(1)}, f32[32,4,1,128]{3,0,2,1:T(8,128)S(1)}, u32[]{:S(2)}, u32[]{:S(2)}) collective-permute-start(f32[32,4,1,128]{3,0,2,1:T(8,128)S(1)} %get-tuple-element.115), channel_id=1, source_target_pairs={{0,16},{16,32},{32,48},{1,17},{17,33},{33,49},{2,18},{18,34},{34,5... | collective-permute-start | bytes 196616 | tf_op jit(solution)/shard_map/ppermute | solution.py:20
  146.1 6.2 collective-permute-start.22
  147.7 5.4 collective-permute-start.23
  153.9 6.5 collective-permute-start.24
  155.2 6.7 collective-permute-start.25
  161.9 17.2 %collective-permute-start.26 = (f32[32,4,1,128]{3,0,2,1:T(8,128)S(1)}, f32[32,4,1,128]{3,0,2,1:T(8,128)S(1)}, u32[]{:S(2)}, u32[]{:S(2)}) collective-permute-start(f32[32,4,1,128]{3,0,2,1:T(8,128)S(1)} %get-tuple-element.114), channel_id=1, source_target_pairs={{16,0},{32,16},{48,32},{17,1},{33,17},{49,33},{18,2},{34,18},{50,3... | collective-permute-start | bytes 196616 | tf_op jit(solution)/shard_map/ppermute | solution.py:23
  163.8 16.4 %collective-permute-start.27 = (f32[32,4,1,128]{3,0,2,1:T(8,128)S(1)}, f32[32,4,1,128]{3,0,2,1:T(8,128)S(1)}, u32[]{:S(2)}, u32[]{:S(2)}) collective-permute-start(f32[32,4,1,128]{3,0,2,1:T(8,128)S(1)} %get-tuple-element.113), channel_id=1, source_target_pairs={{0,16},{16,32},{32,48},{1,17},{17,33},{33,49},{2,18},{18,34},{34,5... | collective-permute-start | bytes 196616 | tf_op jit(solution)/shard_map/ppermute | solution.py:20
  180.8 6.7 collective-permute-start.28
  182.4 5.8 collective-permute-start.29
  189.0 8.7 collective-permute-start.30
  195.5 8.2 collective-permute-start.31
  203.7 17.8 %collective-permute-start.32 = (f32[32,4,1,128]{3,0,2,1:T(8,128)S(1)}, f32[32,4,1,128]{3,0,2,1:T(8,128)S(1)}, u32[]{:S(2)}, u32[]{:S(2)}) collective-permute-start(f32[32,4,1,128]{3,0,2,1:T(8,128)S(1)} %get-tuple-element.112), channel_id=1, source_target_pairs={{0,16},{16,32},{32,48},{1,17},{17,33},{33,49},{2,18},{18,34},{34,5... | collective-permute-start | bytes 196616 | tf_op jit(solution)/shard_map/ppermute | solution.py:20
  218.8 14.7 %collective-permute-start.33 = (f32[32,4,1,128]{3,0,2,1:T(8,128)S(1)}, f32[32,4,1,128]{3,0,2,1:T(8,128)S(1)}, u32[]{:S(2)}, u32[]{:S(2)}) collective-permute-start(f32[32,4,1,128]{3,0,2,1:T(8,128)S(1)} %get-tuple-element.111), channel_id=1, source_target_pairs={{16,0},{32,16},{48,32},{17,1},{33,17},{49,33},{18,2},{34,18},{50,3... | collective-permute-start | bytes 196616 | tf_op jit(solution)/shard_map/ppermute | solution.py:23
  234.1 8.0 collective-permute-start.34
  240.4 7.2 collective-permute-start.35
  547.2 4.0 copy-start
  548.1 331.4 %all-reduce.15.cloned.1.call-start = ((), (), s32[]{:S(2)}) async-start(), calls=%async_computation.3 | async-start | bytes 2621440 | tf_op jit(solution)/shard_map/psum | solution.py:30
  663.5 278.6 %copy-start.3 = (f32[512,256]{0,1:T(8,128)S(1)}, f32[512,256]{0,1:T(8,128)}, u32[]{:S(2)}) copy-start(f32[512,256]{0,1:T(8,128)} %all-reduce.9.cloned.1.call-done) | copy-start | bytes 1572868
  663.5 400.4 %all-reduce.11.cloned.1.call-start = ((), (), s32[]{:S(2)}) async-start(), calls=%async_computation.1 | async-start | bytes 1048576 | tf_op jit(solution)/shard_map/psum | solution.py:30
  903.2 40.1 %copy-start.5 = (f32[256,1024]{1,0:T(8,128)S(1)}, f32[256,1024]{1,0:T(8,128)}, u32[]{:S(2)}) copy-start(f32[256,1024]{1,0:T(8,128)} %get-tuple-element.84) | copy-start | bytes 3145732
  942.8 2.3 copy-start.1
  949.5 331.9 %all-reduce.13.cloned.1.call-start = ((), (), s32[]{:S(2)}) async-start(), calls=%async_computation.2 | async-start | bytes 2621440 | tf_op jit(solution)/shard_map/psum | solution.py:30
  1065.5 278.4 %copy-start.4 = (f32[512,256]{0,1:T(8,128)S(1)}, f32[512,256]{0,1:T(8,128)}, u32[]{:S(2)}) copy-start(f32[512,256]{0,1:T(8,128)} %all-reduce.11.cloned.1.call-done) | copy-start | bytes 1572868
  1343.9 1.3 copy-start.6
Sparse Core Ops, SparseCore 0:
  548.2 113.5 all-reduce.8
  664.2 215.2 all-reduce.14
  949.6 114.1 all-reduce.10
  1066.1 215.2 all-reduce.12
where the time goes:
time: 1370 us; the launch traced here: 1360 us
  waiting for transfers between devices  692 us (51%)
  blocking collectives  263 us (19%)
  starting transfers between devices  173 us (13%)
  other arithmetic  151 us (11%)
  local copies, waits for them, and re-layouts  51.9 us (4%)
  between operations  17.3 us (1%)
  matrix products  15.8 us (1%)
    psum x4, waiting for transfers between devices, from_root(): return lax.psum(kept, axis)  645 us
    all_gather x1, blocking collectives, on_device(): piece = lax.all_gather(blocks[None], ('gx', 'gy'), axis=0, tiled=True)  212 us
    ppermute x18, starting transfers between devices, with_halo(): lax.ppermute(lax.slice_in_dim(block, block.shape[dim] - width, None, axis...  145 us
    another operation x14, other arithmetic, on_device(): factor = jnp.linalg.cholesky(diagonal_piece)  69.3 us
    all_gather x1, blocking collectives, on_device(): lax.all_gather(owned, 'gz', axis=0, tiled=True)  50.5 us
    another operation x5, other arithmetic, on_device(): jax.scipy.linalg.solve_triangular(factor, column_piece.T, lower=True)  39.8 us
    ppermute x18, waiting for transfers between devices, with_halo(): lax.ppermute(lax.slice_in_dim(block, 0, width, axis=dim), axis, backward)  36 us
  transfers between devices with their start and end apart: 40, of which 24 were waited for; matrix products, arithmetic and copies ran while one was open for 2% of the time, Pallas kernels for 0%

commit v1 on v0

--- a/solution.py
+++ b/solution.py
@@ -10,6 +10,12 @@
 upper_edge = 120.0
 lower_edge = 24.0
 coarse_shift = 1.0
+
+
+def add_all(x, axis):
+    shards = lax.all_gather(x, axis, axis=0, tiled=False)
+    total = shards.sum(axis=0)
+    return total
 
 
 def with_halo(block, sides, width):
@@ -27,7 +33,7 @@
 
 def from_root(value, axis, source):
     kept = jnp.where(lax.axis_index(axis) == source, value, 0).astype(value.dtype)
-    return lax.psum(kept, axis)
+    return add_all(kept, axis)
 
 
 def cheb_factors(step_index):

time: 1370 us -> 5790 us (4.23)
  waiting for transfers between devices: 692 us -> 5010 us
    all_gather x0 -> x6, waiting for transfers between devices: none -> 4960 us  [add_all(): shards = lax.all_gather(x, axis, axis=0, tiled=False)]
    psum x4 -> x0, waiting for transfers between devices: 645 us -> none  [from_root(): return lax.psum(kept, axis)]
  transfers between devices with their start and end apart: 40 -> 42, of which waited for: 24 -> 25; matrix products, arithmetic and copies ran while one was open for 2% -> 3% of each run, Pallas kernels for 0% -> 0%
where the time goes in v1:
time: 5790 us; the launch traced here: 5750 us
  waiting for transfers between devices  5010 us (87%)
  blocking collectives  256 us (4%)
  other arithmetic  180 us (3%)
  starting transfers between devices  167 us (3%)
  local copies, waits for them, and re-layouts  108 us (2%)
    all_gather x6, waiting for transfers between devices, add_all(): shards = lax.all_gather(x, axis, axis=0, tiled=False)  4960 us
    all_gather x1, blocking collectives, on_device(): piece = lax.all_gather(blocks[None], ('gx', 'gy'), axis=0, tiled=True)  235 us
    ppermute x18, starting transfers between devices, with_halo(): lax.ppermute(lax.slice_in_dim(block, block.shape[dim] - width, None, axis...  135 us
  transfers between devices with their start and end apart: 42, of which 25 were waited for; matrix products, arithmetic and copies ran while one was open for 3% of the time, Pallas kernels for 0%

profile of v1, /device:TPU:1, one launch (start us, length us, event | category | flops | bytes accessed | tf_op | source)
XLA Modules:
  0.0 5752.1 jit_solution(17542368732654720280)
XLA Ops:
  7.6 4.4 collective-permute-start.7
  15.4 4.8 collective-permute-start.1
  21.5 3.0 select_reduce_fusion.1
  24.6 6.1 collective-permute-start.2
  30.6 11.6 collective-permute-start.3
  43.0 3.1 collective-permute-start.5
  47.5 3.1 collective-permute-done.4
  53.8 14.3 collective-permute-start.9
  70.1 3.1 collective-permute-start.11
  75.2 2.9 collective-permute-done.10
  80.1 4.3 collective-permute-start.13
  88.2 15.5 collective-permute-start.15
  103.7 2.7 collective-permute-done.15
  107.0 4.4 collective-permute-start.17
  118.6 4.0 collective-permute-start.19
  126.5 15.6 collective-permute-start.21
  145.3 3.7 collective-permute-start.23
  151.0 3.2 collective-permute-done.22
  156.2 4.0 collective-permute-start.25
  164.1 15.5 collective-permute-start.27
  181.5 3.7 collective-permute-start.29
  187.3 3.0 collective-permute-done.28
  191.1 4.1 collective-permute-start.30
  197.3 4.5 collective-permute-done.31
  201.8 15.2 collective-permute-start.32
  219.7 12.4 collective-permute-done.33
  232.7 3.7 collective-permute-start.34
  238.6 2.9 collective-permute-done.35
  241.8 234.9 %all-gather = f32[224,32,32]{2,1,0:T(8,128)S(1)} all-gather(f32[7,32,32]{2,1,0:T(8,128)S(1)} %fusion.2), channel_id=2, replica_groups=mesh['gx'=8,'gy'=4,'gz'=16] {'gx','gy'}, dimensions={0}, use_global_device_ids=true | all-gather | bytes 946176 | tf_op jit(solution)/shard_map/all_gather | solution.py:152
  477.2 21.6 all_gather.41
  498.8 4.3 broadcast_in_dim.82
  503.1 19.3 scatter_fusion
  522.5 9.0 copy.208
  531.5 6.2 reshape.418
  538.7 84.4 %all-gather.15.cloned.1.call-done = f32[8192,256]{0,1:T(8,128)} async-done(((f32[512,256]{0,1:T(8,128)}), f32[8192,256]{0,1:T(8,128)}) %all-gather.15.cloned.1.call-update) | async-done | bytes 8388624 | tf_op jit(solution)/shard_map/all_gather | solution.py:16
  623.1 10.9 copy.224
  634.0 3.1 bitcast_reduce_fusion.4
  638.3 3.0 slice_select_fusion
  641.3 4.3 copy.210
  645.7 4.6 select_n.201
  651.0 509.4 %all-gather.17.cloned.1.call-done = f32[8192,256]{0,1:T(8,128)} async-done(((f32[256,256]{0,1:T(8,128)}), f32[8192,256]{0,1:T(8,128)}) %all-gather.17.cloned.1.call-update) | async-done | bytes 8388624 | tf_op jit(solution)/shard_map/all_gather | solution.py:16
  1160.4 6.8 copy.225
  1169.6 11.7 cholesky.130
  1181.3 9.8 custom-call.19
  1191.6 11.7 cholesky.147
  1206.1 3.9 while.10
  1209.9 19.9 custom-call.20
  1231.1 1887.9 %all-gather.13.cloned.1.call-done = f32[32,256,1024]{2,1,0:T(8,128)} async-done(((f32[1,256,1024]{2,1,0:T(8,128)}), f32[32,256,1024]{2,1,0:T(8,128)}) %all-gather.13.cloned.1.call-update) | async-done | bytes 33554448 | tf_op jit(solution)/shard_map/all_gather | solution.py:16
  3119.0 11.8 reduce_sum.119
  3137.5 87.9 %all-gather.19.cloned.1.call-done = f32[8192,256]{0,1:T(8,128)} async-done(((f32[512,256]{0,1:T(8,128)}), f32[8192,256]{0,1:T(8,128)}) %all-gather.19.cloned.1.call-update) | async-done | bytes 8388624 | tf_op jit(solution)/shard_map/all_gather | solution.py:16
  3225.4 10.9 copy.226
  3236.4 3.1 bitcast_reduce_fusion.2
  3242.6 520.1 %all-gather.21.cloned.1.call-done = f32[8192,256]{0,1:T(8,128)} async-done(((f32[256,256]{0,1:T(8,128)}), f32[8192,256]{0,1:T(8,128)}) %all-gather.21.cloned.1.call-update) | async-done | bytes 8388624 | tf_op jit(solution)/shard_map/all_gather | solution.py:16
  3762.7 6.8 copy.227
  3771.9 11.7 cholesky.164
  3783.6 9.8 custom-call.22
  3793.9 11.7 cholesky.181
  3808.2 3.8 while.11
  3812.0 19.9 custom-call.23
  3833.1 1868.7 %all-gather.23.cloned.1.call-done = f32[8192,1024]{0,1:T(8,128)} async-done(((f32[256,1024]{0,1:T(8,128)}), f32[8192,1024]{0,1:T(8,128)}) %all-gather.23.cloned.1.call-update) | async-done | bytes 33554448 | tf_op jit(solution)/shard_map/all_gather | solution.py:16
  5701.8 19.6 copy.228
  5721.4 7.7 bitcast_reduce_fusion
  5734.9 4.6 select_select_fusion
  5742.1 2.9 copy.215
  (235 shorter events, 95.3 us)
Async XLA Ops:
  6.5 616.6 %all-gather.15.cloned.1.call-start = ((), (), s32[]{:S(2)}) async-start(), calls=%async_computation.1 | async-start | bytes 8912896 | tf_op jit(solution)/shard_map/all_gather | solution.py:16
  7.6 43.2 collective-permute-start.7
  12.0 39.9 collective-permute-start.6
  14.1 10.4 collective-permute-start
  15.4 9.1 collective-permute-start.1
  24.6 17.7 collective-permute-start.2
  30.6 12.3 collective-permute-start.3
  43.0 4.5 collective-permute-start.5
  46.2 4.5 collective-permute-start.4
  51.9 16.4 collective-permute-start.8
  53.8 15.6 collective-permute-start.9
  69.8 14.6 copy-start.3
  70.1 4.7 collective-permute-start.11
  73.5 4.5 collective-permute-start.10
  78.8 6.1 collective-permute-start.12
  80.1 6.2 collective-permute-start.13
  84.8 32.0 copy-start.2
  86.3 17.4 collective-permute-start.14
  88.2 18.2 collective-permute-start.15
  107.0 7.2 collective-permute-start.17
  111.7 4.8 collective-permute-start.16
  117.3 5.7 collective-permute-start.18
  118.6 5.9 collective-permute-start.19
  124.6 18.2 collective-permute-start.20
  126.5 18.2 collective-permute-start.21
  145.3 5.4 collective-permute-start.23
  149.3 4.8 collective-permute-start.22
  154.9 5.7 collective-permute-start.24
  156.2 5.9 collective-permute-start.25
  162.1 17.5 collective-permute-start.26
  164.1 16.8 collective-permute-start.27
  181.5 5.5 collective-permute-start.29
  185.5 4.8 collective-permute-start.28
  191.1 6.2 collective-permute-start.30
  195.2 6.6 collective-permute-start.31
  201.8 17.9 collective-permute-start.32
  217.1 15.0 collective-permute-start.33
  232.7 5.7 collective-permute-start.34
  236.7 4.8 collective-permute-start.35
  537.8 96.3 %copy-start = (f32[512,1024]{0,1:T(8,128)}, f32[512,1024]{0,1:T(8,128)S(1)}, u32[]{:S(2)}) copy-start(f32[512,1024]{0,1:T(8,128)S(1)} %reshape.418) | copy-start | bytes 6291460
  538.7 621.8 %all-gather.17.cloned.1.call-start = ((), (), s32[]{:S(2)}) async-start(), calls=%async_computation.2 | async-start | bytes 8650752 | tf_op jit(solution)/shard_map/all_gather | solution.py:16
  637.9 2481.1 %all-gather.13.cloned.1.call-start = ((), (), s32[]{:S(2)}) async-start(), calls=%async_computation | async-start | bytes 34603008 | tf_op jit(solution)/shard_map/all_gather | solution.py:16
  650.3 2575.1 %all-gather.19.cloned.1.call-start = ((), (), s32[]{:S(2)}) async-start(), calls=%async_computation.3 | async-start | bytes 8912896 | tf_op jit(solution)/shard_map/all_gather | solution.py:16
  3130.9 1.9 copy-start.1
  3137.0 625.7 %all-gather.21.cloned.1.call-start = ((), (), s32[]{:S(2)}) async-start(), calls=%async_computation.4 | async-start | bytes 8650752 | tf_op jit(solution)/shard_map/all_gather | solution.py:16
  3240.2 2461.6 %all-gather.23.cloned.1.call-start = ((), (), s32[]{:S(2)}) async-start(), calls=%async_computation.5 | async-start | bytes 34603008 | tf_op jit(solution)/shard_map/all_gather | solution.py:16
Sparse Core Ops, SparseCore 0:
  538.8 84.2 all-gather.14
  638.0 522.4 all-gather.16
  1162.5 1956.4 all-gather.12
  3137.1 88.2 all-gather.18
  3240.3 522.4 all-gather.20
  3764.7 1937.0 all-gather.22
